TPU v7x, 256 devices: a whole 4x4x8 slice. The times are simulated.
256 devices in a mesh: sub: 32 (over z, x), agg: 8 (over y, core).
Axes of the slice: x: 4, y: 4, z: 8, core: 2. Of those that a mesh axis runs over, the one named last changes fastest.
Arguments:
- dual_load: float32 [8, 32, 64, 1536], P('agg', 'sub'), may hold values from -58 to 58
- interface_inverse: bfloat16 [8, 32, 1536, 1536], P('agg', 'sub'), may hold values from -1 to 2.5, as said below
- dirichlet: bfloat16 [8, 32, 1536, 1536], P('agg', 'sub'), may hold values from -1 to 2.5, as said below
- coupling: bfloat16 [8, 32, 128, 1536], P('agg', 'sub'), may hold values from -0.15625 to 0.15625
- neighbours: int32 [8, 32, 8], P('agg', 'sub'), may hold values from -1 to 31, as said below
- face_counts: int32 [8, 32, 8], P('agg', 'sub'), may hold values from 0 to 192, as said below
- owners: int32 [8, 32, 128, 1], P('agg', 'sub'), may hold values from 0 to 7; in each aligned block of 128 rows (0 to 127, 128 to 255, ..., all dimensions but the last counted through in order) at most 48 rows name the same one
- primal_rows: int32 [8, 32, 128], P('agg', 'sub'), may hold values from 0 to 1023
- coarse_inverse: float32 [8, 1024, 1024], P('agg', 'sub'), may hold values from -1 to 1.5, as said below
Outputs:
- solution: float32 [8, 32, 64, 1536], P('agg', 'sub')
- residual: float32 [8, 32, 64, 1536], P('agg', 'sub')
Inputs may be any that keep to these rules, and one draw needn't show every extreme that they name: `neighbours`: each subdomain lists peers of its own aggregate by their index along sub, -1 in empty slots; no peer twice; if j lists i then i lists j; every listed peer lies within a cyclic distance of 4 along sub. `face_counts`: 0 exactly in empty slots, 48 or more elsewhere; both sides of a face give the same count and hold its rows in the same order. `owners`: among the 128 primal rows of one subdomain no aggregate is named more than 48 times. `interface_inverse`: each subdomain's matrix is symmetric positive definite. `dirichlet`: each subdomain's matrix is symmetric positive definite. `coarse_inverse`: each aggregate's matrix is symmetric positive definite.
All inputs are finite; a program needn't handle non-finite values.
Results may differ from a plain program's by a relative error of at most 0.011.
Values sent between devices are 32-bit elements; how exact they have to be, the bound alone decides.
No kernel may reach another device: no remote copies, remote signals or barrier semaphores. Data moves between devices by JAX's collectives and lax.ppermute only.
A program may use at most 128 MiB of HBM per device.

v0:
```python
import jax
import jax.numpy as jnp
from jax import lax
from jax.sharding import PartitionSpec as P

NC = 1024
CAP = 48
ITERS = 2
FULL_PRECISION = lax.Precision.HIGHEST
CONTRACT_LAST = (((1,), (1,)), ((), ()))


def from_behind_2(block, axis, distance):
    devices = range(lax.axis_size(axis))
    route = [((i - distance) % len(devices), i) for i in devices]
    return lax.ppermute(block, axis, route)


def shards(
    dual_load,
    interface_inverse,
    dirichlet,
    coupling,
    neighbours,
    face_counts,
    owners,
    primal_rows,
    coarse_inverse,
):
    inverse_block = interface_inverse[0, 0]
    dirichlet_block = dirichlet[0, 0]
    coupling_block = coupling[0, 0]
    peer_list = neighbours[0, 0]
    count_list = face_counts[0, 0]
    sub_count = lax.axis_size("sub")
    agg_count = lax.axis_size("agg")
    position = lax.axis_index("sub")
    slot_count = peer_list.shape[0]
    inner_order = inverse_block.shape[0]
    face_depth = inner_order // slot_count
    reach = min(4, (sub_count - 1) // 2)
    inside = (
        (jnp.arange(face_depth, dtype=jnp.int32)[None, :] < count_list[:, None])
        .reshape(1, inner_order)
        .astype(jnp.float32)
    )

    def assemble(local):
        case_count = local.shape[0]
        faces = local.reshape(case_count, slot_count, face_depth)
        placed = jnp.zeros_like(faces)
        for distance in range(1, reach + 1):
            ahead = (position + distance) % sub_count
            behind = (position + sub_count - distance) % sub_count
            to_ahead = (peer_list == ahead).astype(jnp.float32)[None, :, None]
            to_behind = (peer_list == behind).astype(jnp.float32)[None, :, None]
            upward = jnp.sum(faces * to_ahead, axis=1)
            downward = jnp.sum(faces * to_behind, axis=1)
            from_behind = from_behind_2(upward, "sub", distance)
            from_ahead = from_behind_2(downward, "sub", -distance)
            placed = (
                placed + to_behind * from_behind[:, None, :] + to_ahead * from_ahead[:, None, :]
            )
        return inside * (local + placed.reshape(case_count, inner_order))

    owner_ids = owners[0, 0, :, 0]
    row_ids = primal_rows[0, 0]
    owner_hot = (owner_ids[:, None] == jnp.arange(agg_count, dtype=jnp.int32)[None, :]).astype(
        jnp.int32
    )
    earlier = jnp.cumsum(owner_hot, axis=0) - owner_hot
    owner_rank = jnp.sum(earlier * owner_hot, axis=1)
    slot_index = owner_ids * CAP + owner_rank
    packing = slot_index[:, None] == jnp.arange(agg_count * CAP, dtype=jnp.int32)[None, :]
    packing_float = packing.astype(jnp.float32)
    sent_rows = jnp.sum(packing.astype(jnp.int32) * (row_ids[:, None] + 1), axis=0) - 1
    got_rows = lax.all_to_all(sent_rows, "agg", split_axis=0, concat_axis=0, tiled=True)
    scatter_hot = (got_rows[:, None] == jnp.arange(NC, dtype=jnp.int32)[None, :]).astype(
        jnp.float32
    )
    inverse_rows = coarse_inverse[0]

    def precondition(field):
        packed = field.astype(jnp.bfloat16)
        return assemble(
            inside * jnp.dot(packed, dirichlet_block, preferred_element_type=jnp.float32)
        )

    def residual_norm(first, second):
        return lax.psum(jnp.sum(first * second, axis=1), ("sub", "agg"))

    rhs = assemble(inside * dual_load[0, 0])
    solution = jnp.zeros_like(rhs)
    residual = rhs
    precond = precondition(residual)
    direction = precond
    residual_dot = residual_norm(residual, precond)
    for iteration in range(ITERS):
        operator_packed = direction.astype(jnp.bfloat16)
        own = jnp.dot(operator_packed, inverse_block, preferred_element_type=jnp.float32)
        terms = lax.dot_general(
            operator_packed, coupling_block, CONTRACT_LAST, preferred_element_type=jnp.float32
        )
        outgoing = jnp.dot(terms, packing_float, precision=FULL_PRECISION)
        gathered = jnp.dot(
            lax.all_to_all(outgoing, "agg", split_axis=1, concat_axis=1, tiled=True),
            scatter_hot,
            precision=FULL_PRECISION,
        )
        coarse_rhs = lax.psum(gathered, "sub")
        partial_rows = lax.dot_general(
            coarse_rhs, inverse_rows, CONTRACT_LAST, precision=FULL_PRECISION
        )
        coarse_sol = lax.all_gather(partial_rows, "sub", axis=1, tiled=True)
        answer = lax.dot_general(coarse_sol, scatter_hot, CONTRACT_LAST, precision=FULL_PRECISION)
        returned = lax.all_to_all(answer, "agg", split_axis=1, concat_axis=1, tiled=True)
        local_back = lax.dot_general(
            returned, packing_float, CONTRACT_LAST, precision=FULL_PRECISION
        )
        correction = jnp.dot(
            local_back.astype(jnp.bfloat16), coupling_block, preferred_element_type=jnp.float32
        )
        image = assemble(inside * (own + correction))
        alpha = (residual_dot / lax.psum(jnp.sum(direction * image, axis=1), ("sub", "agg")))[
            :, None
        ]
        solution = solution + alpha * direction
        residual = residual - alpha * image
        if iteration + 1 < ITERS:
            precond = precondition(residual)
            next_dot = residual_norm(residual, precond)
            direction = precond + (next_dot / residual_dot)[:, None] * direction
            residual_dot = next_dot
    return (solution[None, None], residual[None, None])


def solution(mesh):
    in_specs = (
        P("agg", "sub", None, None),
        P("agg", "sub", None, None),
        P("agg", "sub", None, None),
        P("agg", "sub", None, None),
        P("agg", "sub", None),
        P("agg", "sub", None),
        P("agg", "sub", None, None),
        P("agg", "sub", None),
        P("agg", "sub", None),
    )
    out_specs = (P("agg", "sub", None, None), P("agg", "sub", None, None))
    return jax.shard_map(shards, mesh=mesh, in_specs=in_specs, out_specs=out_specs, check_vma=False)
```

profile of v0, /device:TPU:1, one launch (start us, length us, event | category | flops | bytes accessed | tf_op | source)
XLA Modules:
  0.0 917.8 jit_solution(6425770265424465426)
XLA Ops:
  11.5 2.1 collective-permute-start
  13.6 6.6 collective-permute-start.1
  20.4 2.7 collective-permute-start.7
  26.0 2.5 collective-permute-start.2
  28.4 2.6 collective-permute-start.3
  41.5 2.0 mul.1238
  45.2 2.0 mul.1235
  48.8 1.9 mul.1232
  50.8 5.2 fusion.8
  56.0 2.0 reshape.646
  58.0 2.5 multiply_reduce_fusion.31
  60.5 4.7 collective-permute-start.11
  65.2 2.7 collective-permute-start.9
  76.5 10.1 %all-to-all-start.1 = ((s32[8,48,1]{1,2,0:T(1,128)}), s32[8,48,1]{1,2,0:T(1,128)}, u32[]{:S(2)}, u32[]{:S(2)}) async-start(s32[8,48,1]{1,2,0:T(1,128)} %bitcast.111), calls=%async_computation.1 | async-start | bytes 8192 | tf_op jit(solution)/shard_map/all_to_all | solution.py:77
  88.4 2.0 mul.1263
  92.0 2.0 mul.1267
  94.8 2.0 mul.1271
  98.5 2.0 mul.1275
  102.1 1.9 mul.1279
  105.8 2.0 mul.1283
  108.6 2.0 mul.1287
  111.4 2.0 mul.1259
  113.4 2.3 add_multiply_fusion.3
  116.0 1.7 fusion.47
  117.7 1.7 reshape.668
  119.4 4.8 all-to-all-start
  124.8 1.9 reduce.3
  129.8 2.4 reduce.4
  133.9 2.4 fusion.29
  136.4 138.3 %all-reduce.4.cloned.1.call-done = f32[64,1024]{1,0:T(8,128)} async-done(((f32[64,1024]{1,0:T(8,128)}), f32[64,1024]{1,0:T(8,128)}) %all-reduce.4.cloned.1.call-update) | async-done | bytes 262160 | tf_op jit(solution)/shard_map/psum | solution.py:110
  275.9 35.9 %all_gather.6 = f32[64,1024]{0,1:T(8,128)S(1)} all-gather(f32[64,32]{0,1:T(8,128)S(1)} %fusion.58), channel_id=1, replica_groups=mesh['sub'=32,'agg'=8] {'sub'}, dimensions={1}, use_global_device_ids=true | all-gather | bytes 270336 | tf_op jit(solution)/shard_map/all_gather | solution.py:114
  311.8 2.3 fusion.28
  314.1 1.7 reshape.670
  315.8 26.7 %all_to_all.54 = f32[8,1,3072]{2,1,0:T(1,128)} all-to-all(f32[8,1,3072]{2,1,0:T(1,128)} %reshape.670), channel_id=1, replica_groups=mesh['sub'=32,'agg'=8] {'agg'}, dimensions={0} | all-to-all | bytes 196608 | tf_op jit(solution)/shard_map/all_to_all | solution.py:116
  342.5 2.4 reduce.5
  348.1 4.0 fusion.23
  352.1 2.0 reshape.647
  354.1 3.2 multiply_reduce_fusion.23
  357.3 2.0 collective-permute-start.19
  360.2 4.5 collective-permute-start.17
  364.7 3.8 collective-permute-start.21
  368.5 2.7 collective-permute-start.23
  375.8 2.0 mul.1186
  394.4 3.9 multiply_reduce_fusion.42
  398.5 77.6 %all-reduce = (f32[64]{0:T(128)S(1)}, f32[64]{0:T(128)S(1)}) all-reduce(f32[64]{0:T(128)S(1)} %get-tuple-element.43, f32[64]{0:T(128)S(1)} %get-tuple-element.42), channel_id=1, replica_groups=mesh['sub'=32,'agg'=8] {'sub','agg'}, use_global_device_ids=true, to_apply=%region_17.18 | all-reduce | flops 128 | bytes 1024 | tf_op jit(solution)/shard_map/psum | solution.py:90
  477.2 3.3 fusion.11
  480.7 1.9 multiply_reduce_fusion.15
  483.4 2.2 collective-permute-start.26
  485.6 2.5 collective-permute-start.25
  488.2 3.5 collective-permute-start.29
  491.7 2.7 collective-permute-start.31
  504.1 1.8 multiply_reduce_fusion.41
  505.9 77.6 %psum.45 = f32[64]{0:T(128)S(1)} all-reduce(f32[64]{0:T(128)S(1)} %get-tuple-element.48), channel_id=1, replica_groups=mesh['sub'=32,'agg'=8] {'sub','agg'}, use_global_device_ids=true, to_apply=%region_41.42 | all-reduce | flops 64 | bytes 512 | tf_op jit(solution)/shard_map/psum | solution.py:90
  585.7 8.1 all_to_all.55
  596.3 136.3 %all-reduce.6.cloned.1.call-done = f32[64,1024]{1,0:T(8,128)} async-done(((f32[64,1024]{1,0:T(8,128)}), f32[64,1024]{1,0:T(8,128)}) %all-reduce.6.cloned.1.call-update) | async-done | bytes 262160 | tf_op jit(solution)/shard_map/psum | solution.py:110
  733.9 35.9 %all_gather.7 = f32[64,1024]{0,1:T(8,128)S(1)} all-gather(f32[64,32]{0,1:T(8,128)S(1)} %fusion.56), channel_id=1, replica_groups=mesh['sub'=32,'agg'=8] {'sub'}, dimensions={1}, use_global_device_ids=true | all-gather | bytes 270336 | tf_op jit(solution)/shard_map/all_gather | solution.py:114
  770.8 26.7 %all_to_all.56 = f32[8,1,3072]{2,1,0:T(1,128)S(1)} all-to-all(f32[8,1,3072]{2,1,0:T(1,128)S(1)} %reshape.674), channel_id=1, replica_groups=mesh['sub'=32,'agg'=8] {'agg'}, dimensions={0} | all-to-all | bytes 196608 | tf_op jit(solution)/shard_map/all_to_all | solution.py:116
  799.1 3.3 fusion.20
  804.3 2.0 collective-permute-start.35
  807.2 4.5 collective-permute-start.33
  811.7 3.6 collective-permute-start.37
  815.3 2.7 collective-permute-start.39
  829.3 2.0 multiply_reduce_fusion.40
  831.3 77.7 %psum.47 = f32[64]{0:T(128)S(1)} all-reduce(f32[64]{0:T(128)S(1)} %get-tuple-element.46), channel_id=1, replica_groups=mesh['sub'=32,'agg'=8] {'sub','agg'}, use_global_device_ids=true, to_apply=%region_52.53 | all-reduce | flops 64 | bytes 512 | tf_op jit(solution)/shard_map/psum | solution.py:124
  (315 shorter events, 108.8 us)
Async XLA Ops:
  7.2 108.6 %copy-start = (bf16[1,1,128,1536]{3,2,1,0:T(8,128)(2,1)S(1)}, bf16[1,1,128,1536]{3,2,1,0:T(8,128)(2,1)}, u32[]{:S(2)}) copy-start(bf16[1,1,128,1536]{3,2,1,0:T(8,128)(2,1)} %param.12) | copy-start | bytes 1179652
  11.5 35.6 %collective-permute-start = (f32[64,192]{1,0:T(8,128)S(1)}, f32[64,192]{1,0:T(8,128)}, u32[]{:S(2)}, u32[]{:S(2)}) collective-permute-start(f32[64,192]{1,0:T(8,128)S(1)} %get-tuple-element.2), channel_id=1, source_target_pairs={{248,0},{0,8},{8,16},{16,24},{24,32},{32,40},{40,48},{48,56},{56,6... | collective-permute-start | bytes 147464 | tf_op jit(solution)/shard_map/ppermute | solution.py:16
  13.6 29.9 %collective-permute-start.1 = (f32[64,192]{1,0:T(8,128)}, f32[64,192]{1,0:T(8,128)}, u32[]{:S(2)}, u32[]{:S(2)}) collective-permute-start(f32[64,192]{1,0:T(8,128)} %get-tuple-element.3), channel_id=1, source_target_pairs={{8,0},{16,8},{24,16},{32,24},{40,32},{48,40},{56,48},{64,56},{72,6... | collective-permute-start | bytes 147464 | tf_op jit(solution)/shard_map/ppermute | solution.py:16
  20.3 5.7 collective-permute-start.5
  20.4 8.1 collective-permute-start.6
  20.4 10.7 %collective-permute-start.7 = (f32[64,192]{1,0:T(8,128)S(1)}, f32[64,192]{1,0:T(8,128)S(1)}, u32[]{:S(2)}, u32[]{:S(2)}) collective-permute-start(f32[64,192]{1,0:T(8,128)S(1)} %get-tuple-element.9), channel_id=1, source_target_pairs={{32,0},{40,8},{48,16},{56,24},{64,32},{72,40},{80,48},{88,56},{96,... | collective-permute-start | bytes 147464 | tf_op jit(solution)/shard_map/ppermute | solution.py:16
  26.0 13.9 %collective-permute-start.2 = (f32[64,192]{1,0:T(8,128)}, f32[64,192]{1,0:T(8,128)}, u32[]{:S(2)}, u32[]{:S(2)}) collective-permute-start(f32[64,192]{1,0:T(8,128)} %get-tuple-element.4), channel_id=1, source_target_pairs={{240,0},{248,8},{0,16},{8,24},{16,32},{24,40},{32,48},{40,56},{48,... | collective-permute-start | bytes 147464 | tf_op jit(solution)/shard_map/ppermute | solution.py:16
  28.4 9.6 %collective-permute-start.3 = (f32[64,192]{1,0:T(8,128)S(1)}, f32[64,192]{1,0:T(8,128)}, u32[]{:S(2)}, u32[]{:S(2)}) collective-permute-start(f32[64,192]{1,0:T(8,128)S(1)} %get-tuple-element.5), channel_id=1, source_target_pairs={{16,0},{24,8},{32,16},{40,24},{48,32},{56,40},{64,48},{72,56},{80,... | collective-permute-start | bytes 147464 | tf_op jit(solution)/shard_map/ppermute | solution.py:16
  31.1 6.0 collective-permute-start.4
  60.5 8.4 collective-permute-start.11
  65.2 6.7 collective-permute-start.10
  65.2 8.3 collective-permute-start.9
  68.6 41.9 %collective-permute-start.8 = (f32[64,192]{1,0:T(8,128)S(1)}, f32[64,192]{1,0:T(8,128)S(1)}, u32[]{:S(2)}, u32[]{:S(2)}) collective-permute-start(f32[64,192]{1,0:T(8,128)S(1)} %get-tuple-element.34), channel_id=1, source_target_pairs={{248,0},{0,8},{8,16},{16,24},{24,32},{32,40},{40,48},{48,56},{56,6... | collective-permute-start | bytes 147464 | tf_op jit(solution)/shard_map/ppermute | solution.py:16
  68.7 39.0 %collective-permute-start.15 = (f32[64,192]{1,0:T(8,128)S(1)}, f32[64,192]{1,0:T(8,128)S(1)}, u32[]{:S(2)}, u32[]{:S(2)}) collective-permute-start(f32[64,192]{1,0:T(8,128)S(1)} %get-tuple-element.35), channel_id=1, source_target_pairs={{32,0},{40,8},{48,16},{56,24},{64,32},{72,40},{80,48},{88,56},{96,... | collective-permute-start | bytes 147464 | tf_op jit(solution)/shard_map/ppermute | solution.py:16
  68.8 35.2 %collective-permute-start.14 = (f32[64,192]{1,0:T(8,128)S(1)}, f32[64,192]{1,0:T(8,128)}, u32[]{:S(2)}, u32[]{:S(2)}) collective-permute-start(f32[64,192]{1,0:T(8,128)S(1)} %get-tuple-element.36), channel_id=1, source_target_pairs={{224,0},{232,8},{240,16},{248,24},{0,32},{8,40},{16,48},{24,56},{3... | collective-permute-start | bytes 147464 | tf_op jit(solution)/shard_map/ppermute | solution.py:16
  71.9 28.5 %collective-permute-start.13 = (f32[64,192]{1,0:T(8,128)S(1)}, f32[64,192]{1,0:T(8,128)}, u32[]{:S(2)}, u32[]{:S(2)}) collective-permute-start(f32[64,192]{1,0:T(8,128)S(1)} %get-tuple-element.37), channel_id=1, source_target_pairs={{24,0},{32,8},{40,16},{48,24},{56,32},{64,40},{72,48},{80,56},{88,... | collective-permute-start | bytes 147464 | tf_op jit(solution)/shard_map/ppermute | solution.py:16
  73.5 23.3 %collective-permute-start.12 = (f32[64,192]{1,0:T(8,128)S(1)}, f32[64,192]{1,0:T(8,128)}, u32[]{:S(2)}, u32[]{:S(2)}) collective-permute-start(f32[64,192]{1,0:T(8,128)S(1)} %get-tuple-element.38), channel_id=1, source_target_pairs={{232,0},{240,8},{248,16},{0,24},{8,32},{16,40},{24,48},{32,56},{40... | collective-permute-start | bytes 147464 | tf_op jit(solution)/shard_map/ppermute | solution.py:16
  76.5 42.9 %all-to-all-start.1 = ((s32[8,48,1]{1,2,0:T(1,128)}), s32[8,48,1]{1,2,0:T(1,128)}, u32[]{:S(2)}, u32[]{:S(2)}) async-start(s32[8,48,1]{1,2,0:T(1,128)} %bitcast.111), calls=%async_computation.1 | async-start | bytes 8192 | tf_op jit(solution)/shard_map/all_to_all | solution.py:77
  108.6 166.1 %copy-start.9 = (f32[1,32,1024]{2,1,0:T(8,128)S(1)}, f32[1,32,1024]{2,1,0:T(8,128)}, u32[]{:S(2)}) copy-start(f32[1,32,1024]{2,1,0:T(8,128)} %param.17) | copy-start | bytes 393220
  119.4 9.9 %all-to-all-start = ((f32[8,1,3072]{2,1,0:T(1,128)}), f32[8,1,3072]{2,1,0:T(1,128)}, u32[]{:S(2)}, u32[]{:S(2)}) async-start(f32[8,1,3072]{2,1,0:T(1,128)} %reshape.668), calls=%async_computation | async-start | bytes 196608 | tf_op jit(solution)/shard_map/all_to_all | solution.py:106
  124.2 150.4 %all-reduce.4.cloned.1.call-start = ((), (), s32[]{:S(2)}) async-start(), calls=%async_computation.5 | async-start | bytes 524288 | tf_op jit(solution)/shard_map/psum | solution.py:110
  136.3 596.3 %all-reduce.6.cloned.1.call-start = ((), (), s32[]{:S(2)}) async-start(), calls=%async_computation.6 | async-start | bytes 524288 | tf_op jit(solution)/shard_map/psum | solution.py:110
  357.3 11.3 %collective-permute-start.19 = (f32[64,192]{1,0:T(8,128)S(1)}, f32[64,192]{1,0:T(8,128)}, u32[]{:S(2)}, u32[]{:S(2)}) collective-permute-start(f32[64,192]{1,0:T(8,128)S(1)} %get-tuple-element.31), channel_id=1, source_target_pairs={{16,0},{24,8},{32,16},{40,24},{48,32},{56,40},{64,48},{72,56},{80,... | collective-permute-start | bytes 147464 | tf_op jit(solution)/shard_map/ppermute | solution.py:16
  359.2 9.3 %collective-permute-start.18 = (f32[64,192]{1,0:T(8,128)S(1)}, f32[64,192]{1,0:T(8,128)}, u32[]{:S(2)}, u32[]{:S(2)}) collective-permute-start(f32[64,192]{1,0:T(8,128)S(1)} %get-tuple-element.32), channel_id=1, source_target_pairs={{240,0},{248,8},{0,16},{8,24},{16,32},{24,40},{32,48},{40,56},{48,... | collective-permute-start | bytes 147464 | tf_op jit(solution)/shard_map/ppermute | solution.py:16
  360.2 11.0 %collective-permute-start.17 = (f32[64,192]{1,0:T(8,128)S(1)}, f32[64,192]{1,0:T(8,128)}, u32[]{:S(2)}, u32[]{:S(2)}) collective-permute-start(f32[64,192]{1,0:T(8,128)S(1)} %get-tuple-element.33), channel_id=1, source_target_pairs={{8,0},{16,8},{24,16},{32,24},{40,32},{48,40},{56,48},{64,56},{72,6... | collective-permute-start | bytes 147464 | tf_op jit(solution)/shard_map/ppermute | solution.py:16
  364.7 20.5 %collective-permute-start.20 = (f32[64,192]{1,0:T(8,128)}, f32[64,192]{1,0:T(8,128)}, u32[]{:S(2)}, u32[]{:S(2)}) collective-permute-start(f32[64,192]{1,0:T(8,128)} %get-tuple-element.30), channel_id=1, source_target_pairs={{232,0},{240,8},{248,16},{0,24},{8,32},{16,40},{24,48},{32,56},{40... | collective-permute-start | bytes 147464 | tf_op jit(solution)/shard_map/ppermute | solution.py:16
  364.7 22.3 %collective-permute-start.21 = (f32[64,192]{1,0:T(8,128)}, f32[64,192]{1,0:T(8,128)}, u32[]{:S(2)}, u32[]{:S(2)}) collective-permute-start(f32[64,192]{1,0:T(8,128)} %get-tuple-element.29), channel_id=1, source_target_pairs={{24,0},{32,8},{40,16},{48,24},{56,32},{64,40},{72,48},{80,56},{88,... | collective-permute-start | bytes 147464 | tf_op jit(solution)/shard_map/ppermute | solution.py:16
  368.5 20.4 %collective-permute-start.22 = (f32[64,192]{1,0:T(8,128)}, f32[64,192]{1,0:T(8,128)}, u32[]{:S(2)}, u32[]{:S(2)}) collective-permute-start(f32[64,192]{1,0:T(8,128)} %get-tuple-element.28), channel_id=1, source_target_pairs={{224,0},{232,8},{240,16},{248,24},{0,32},{8,40},{16,48},{24,56},{3... | collective-permute-start | bytes 147464 | tf_op jit(solution)/shard_map/ppermute | solution.py:16
  368.5 22.2 %collective-permute-start.23 = (f32[64,192]{1,0:T(8,128)}, f32[64,192]{1,0:T(8,128)}, u32[]{:S(2)}, u32[]{:S(2)}) collective-permute-start(f32[64,192]{1,0:T(8,128)} %get-tuple-element.27), channel_id=1, source_target_pairs={{32,0},{40,8},{48,16},{56,24},{64,32},{72,40},{80,48},{88,56},{96,... | collective-permute-start | bytes 147464 | tf_op jit(solution)/shard_map/ppermute | solution.py:16
  371.2 21.3 %collective-permute-start.16 = (f32[64,192]{1,0:T(8,128)}, f32[64,192]{1,0:T(8,128)}, u32[]{:S(2)}, u32[]{:S(2)}) collective-permute-start(f32[64,192]{1,0:T(8,128)} %get-tuple-element.26), channel_id=1, source_target_pairs={{248,0},{0,8},{8,16},{16,24},{24,32},{32,40},{40,48},{48,56},{56,6... | collective-permute-start | bytes 147464 | tf_op jit(solution)/shard_map/ppermute | solution.py:16
  398.4 82.3 %copy-start.29 = (f32[8]{0:T(128)S(1)}, f32[8]{0:T(128)}, u32[]{:S(2)}) copy-start(f32[8]{0:T(128)} %copy-done.28) | copy-start | bytes 100
  398.4 82.3 %copy-start.31 = (f32[8]{0:T(128)S(1)}, f32[8]{0:T(128)}, u32[]{:S(2)}) copy-start(f32[8]{0:T(128)} %copy-done.30) | copy-start | bytes 100
  398.4 82.3 %copy-start.34 = (f32[8]{0:T(128)S(1)}, f32[8]{0:T(128)}, u32[]{:S(2)}) copy-start(f32[8]{0:T(128)} %copy-done.33) | copy-start | bytes 100
  398.4 82.3 %copy-start.37 = (f32[8]{0:T(128)S(1)}, f32[8]{0:T(128)}, u32[]{:S(2)}) copy-start(f32[8]{0:T(128)} %copy-done.36) | copy-start | bytes 100
  398.4 82.3 %copy-start.40 = (f32[8]{0:T(128)S(1)}, f32[8]{0:T(128)}, u32[]{:S(2)}) copy-start(f32[8]{0:T(128)} %copy-done.39) | copy-start | bytes 100
  398.4 82.3 %copy-start.43 = (f32[8]{0:T(128)S(1)}, f32[8]{0:T(128)}, u32[]{:S(2)}) copy-start(f32[8]{0:T(128)} %copy-done.42) | copy-start | bytes 100
  398.4 82.3 %copy-start.46 = (f32[8]{0:T(128)S(1)}, f32[8]{0:T(128)}, u32[]{:S(2)}) copy-start(f32[8]{0:T(128)} %copy-done.45) | copy-start | bytes 100
  398.5 82.3 %copy-start.49 = (f32[8]{0:T(128)S(1)}, f32[8]{0:T(128)}, u32[]{:S(2)}) copy-start(f32[8]{0:T(128)} %copy-done.48) | copy-start | bytes 100
  482.7 9.0 collective-permute-start.27
  483.4 8.2 collective-permute-start.26
  485.6 8.7 collective-permute-start.25
  488.1 6.9 collective-permute-start.28
  488.2 8.7 collective-permute-start.29
  491.7 7.0 collective-permute-start.30
  491.7 8.8 collective-permute-start.31
  494.4 7.9 collective-permute-start.24
  502.3 92.5 %copy-start.27 = (s32[384]{0:T(512)S(1)}, s32[384]{0:T(512)}, u32[]{:S(2)}) copy-start(s32[384]{0:T(512)} %eq.256) | copy-start | bytes 4612
  504.1 294.4 %copy-start.51 = (s32[128]{0:T(128)S(1)}, s32[128]{0:T(128)}, u32[]{:S(2)}) copy-start(s32[128]{0:T(128)} %multiply_add_fusion.1) | copy-start | bytes 1540
  583.5 218.8 %copy-start.54 = (f32[64]{0:T(128)}, f32[64]{0:T(128)S(1)}, u32[]{:S(2)}) copy-start(f32[64]{0:T(128)S(1)} %psum.45) | copy-start | bytes 772
  769.7 32.8 %copy-start.35 = (f32[8]{0:T(128)S(1)}, f32[8]{0:T(128)}, u32[]{:S(2)}) copy-start(f32[8]{0:T(128)} %copy-done.33) | copy-start | bytes 100
  769.7 32.8 %copy-start.38 = (f32[8]{0:T(128)S(1)}, f32[8]{0:T(128)}, u32[]{:S(2)}) copy-start(f32[8]{0:T(128)} %copy-done.36) | copy-start | bytes 100
  769.7 32.8 %copy-start.41 = (f32[8]{0:T(128)S(1)}, f32[8]{0:T(128)}, u32[]{:S(2)}) copy-start(f32[8]{0:T(128)} %copy-done.39) | copy-start | bytes 100
  769.8 32.8 %copy-start.44 = (f32[8]{0:T(128)S(1)}, f32[8]{0:T(128)}, u32[]{:S(2)}) copy-start(f32[8]{0:T(128)} %copy-done.42) | copy-start | bytes 100
  769.8 32.8 %copy-start.47 = (f32[8]{0:T(128)S(1)}, f32[8]{0:T(128)}, u32[]{:S(2)}) copy-start(f32[8]{0:T(128)} %copy-done.45) | copy-start | bytes 100
  769.8 32.8 %copy-start.50 = (f32[8]{0:T(128)S(1)}, f32[8]{0:T(128)}, u32[]{:S(2)}) copy-start(f32[8]{0:T(128)} %copy-done.48) | copy-start | bytes 100
  804.3 11.0 %collective-permute-start.35 = (f32[64,192]{1,0:T(8,128)S(1)}, f32[64,192]{1,0:T(8,128)S(1)}, u32[]{:S(2)}, u32[]{:S(2)}) collective-permute-start(f32[64,192]{1,0:T(8,128)S(1)} %get-tuple-element.15), channel_id=1, source_target_pairs={{16,0},{24,8},{32,16},{40,24},{48,32},{56,40},{64,48},{72,56},{80,... | collective-permute-start | bytes 147464 | tf_op jit(solution)/shard_map/ppermute | solution.py:16
  806.2 9.1 collective-permute-start.34
  807.2 10.8 %collective-permute-start.33 = (f32[64,192]{1,0:T(8,128)S(1)}, f32[64,192]{1,0:T(8,128)S(1)}, u32[]{:S(2)}, u32[]{:S(2)}) collective-permute-start(f32[64,192]{1,0:T(8,128)S(1)} %get-tuple-element.17), channel_id=1, source_target_pairs={{8,0},{16,8},{24,16},{32,24},{40,32},{48,40},{56,48},{64,56},{72,6... | collective-permute-start | bytes 147464 | tf_op jit(solution)/shard_map/ppermute | solution.py:16
  811.7 8.5 collective-permute-start.36
  811.7 10.3 %collective-permute-start.37 = (f32[64,192]{1,0:T(8,128)}, f32[64,192]{1,0:T(8,128)}, u32[]{:S(2)}, u32[]{:S(2)}) collective-permute-start(f32[64,192]{1,0:T(8,128)} %get-tuple-element.13), channel_id=1, source_target_pairs={{24,0},{32,8},{40,16},{48,24},{56,32},{64,40},{72,48},{80,56},{88,... | collective-permute-start | bytes 147464 | tf_op jit(solution)/shard_map/ppermute | solution.py:16
  815.3 8.6 collective-permute-start.38
  815.3 10.3 %collective-permute-start.39 = (f32[64,192]{1,0:T(8,128)S(1)}, f32[64,192]{1,0:T(8,128)}, u32[]{:S(2)}, u32[]{:S(2)}) collective-permute-start(f32[64,192]{1,0:T(8,128)S(1)} %get-tuple-element.11), channel_id=1, source_target_pairs={{32,0},{40,8},{48,16},{56,24},{64,32},{72,40},{80,48},{88,56},{96,... | collective-permute-start | bytes 147464 | tf_op jit(solution)/shard_map/ppermute | solution.py:16
  818.0 9.5 %collective-permute-start.32 = (f32[64,192]{1,0:T(8,128)S(1)}, f32[64,192]{1,0:T(8,128)}, u32[]{:S(2)}, u32[]{:S(2)}) collective-permute-start(f32[64,192]{1,0:T(8,128)S(1)} %get-tuple-element.10), channel_id=1, source_target_pairs={{248,0},{0,8},{8,16},{16,24},{24,32},{32,40},{40,48},{48,56},{56,6... | collective-permute-start | bytes 147464 | tf_op jit(solution)/shard_map/ppermute | solution.py:16
  822.9 86.6 %copy-start.53 = (f32[64]{0:T(128)S(1)}, f32[64]{0:T(128)}, u32[]{:S(2)}) copy-start(f32[64]{0:T(128)} %copy-done.52) | copy-start | bytes 772
  (36 other events, 519.4 us)
Sparse Core Ops, SparseCore 0:
  136.4 138.1 all-reduce.3
  596.4 136.1 all-reduce.5
where the time goes:
time: 927 us; the launch traced here: 918 us
  blocking collectives  366 us (39%)
  waiting for transfers between devices  278 us (30%)
  local copies, waits for them, and re-layouts  105 us (11%)
  starting transfers between devices  83.3 us (9%)
  other arithmetic  39.7 us (4%)
  matrix products  30.5 us (3%)
  between operations  15.6 us (2%)
    psum x2, waiting for transfers between devices, shards(): coarse_rhs = lax.psum(gathered, 'sub')  275 us
    psum x2, blocking collectives, residual_norm(): return lax.psum(jnp.sum(first * second, axis=1), ('sub', 'agg'))  155 us
    psum x1, blocking collectives, shards(): lax.psum(jnp.sum(direction * image, axis=1), ('sub', 'agg'))  77.7 us
    all_gather x2, blocking collectives, shards(): coarse_sol = lax.all_gather(partial_rows, 'sub', axis=1, tiled=True)  71.7 us
    ppermute x40, starting transfers between devices, from_behind_2(): return lax.ppermute(block, axis, route)  68.3 us
    all_to_all x2, blocking collectives, shards(): lax.all_to_all(answer, 'agg', split_axis=1, concat_axis=1, tiled=True)  53.4 us
    mul x52, local copies, waits for them, and re-layouts, assemble(): to_behind * from_behind[:, None, :]  46.7 us
    mul x44, local copies, waits for them, and re-layouts, assemble(): to_ahead * from_ahead[:, None, :]  40.9 us
  transfers between devices with their start and end apart: 44, of which 4 were waited for; matrix products, arithmetic and copies ran while one was open for 10% of the time, Pallas kernels for 0%

commit v1 on v0

--- a/solution.py
+++ b/solution.py
@@ -111,7 +111,10 @@
         partial_rows = lax.dot_general(
             coarse_rhs, inverse_rows, CONTRACT_LAST, precision=FULL_PRECISION
         )
-        coarse_sol = lax.all_gather(partial_rows, "sub", axis=1, tiled=True)
+        count = lax.axis_size("sub")
+        blocks = jnp.stack([partial_rows for _ in range(count)])
+        blocks = lax.all_to_all(blocks, "sub", split_axis=0, concat_axis=0)
+        coarse_sol = jnp.concatenate(blocks, axis=1)
         answer = lax.dot_general(coarse_sol, scatter_hot, CONTRACT_LAST, precision=FULL_PRECISION)
         returned = lax.all_to_all(answer, "agg", split_axis=1, concat_axis=1, tiled=True)
         local_back = lax.dot_general(

time: 927 us -> 873 us (0.942)
  blocking collectives: 366 us -> 304 us
    all_gather x2 -> x0, blocking collectives: 71.7 us -> none  [shards(): coarse_sol = lax.all_gather(partial_rows, 'sub', axis=1, tiled=True)]
    all_to_all x0 -> x2, blocking collectives: none -> 30.6 us  [shards(): blocks = lax.all_to_all(blocks, 'sub', split_axis=0, concat_axis=0)]
    all_to_all x2, blocking collectives: 53.4 us -> 32.5 us  [shards(): lax.all_to_all(answer, 'agg', split_axis=1, concat_axis=1, tiled=True)]
  transfers between devices with their start and end apart: 44 -> 44, of which waited for: 4 -> 4; matrix products, arithmetic and copies ran while one was open for 10% -> 11% of each run, Pallas kernels for 0% -> 0%
where the time goes in v1:
time: 873 us; the launch traced here: 863 us
  blocking collectives  304 us (35%)
  waiting for transfers between devices  278 us (32%)
  local copies, waits for them, and re-layouts  110 us (13%)
  starting transfers between devices  79.8 us (9%)
  other arithmetic  43.4 us (5%)
  matrix products  31.6 us (4%)
  between operations  15.4 us (2%)
    psum x2, waiting for transfers between devices, shards(): coarse_rhs = lax.psum(gathered, 'sub')  275 us
    psum x2, blocking collectives, residual_norm(): return lax.psum(jnp.sum(first * second, axis=1), ('sub', 'agg'))  155 us
    psum x1, blocking collectives, shards(): lax.psum(jnp.sum(direction * image, axis=1), ('sub', 'agg'))  77.8 us
    ppermute x40, starting transfers between devices, from_behind_2(): return lax.ppermute(block, axis, route)  64.7 us
    mul x52, local copies, waits for them, and re-layouts, assemble(): to_behind * from_behind[:, None, :]  46.7 us
    mul x44, local copies, waits for them, and re-layouts, assemble(): to_ahead * from_ahead[:, None, :]  40.9 us
    all_to_all x2, blocking collectives, shards(): lax.all_to_all(answer, 'agg', split_axis=1, concat_axis=1, tiled=True)  32.5 us
    all_to_all x2, blocking collectives, shards(): blocks = lax.all_to_all(blocks, 'sub', split_axis=0, concat_axis=0)  30.6 us
  transfers between devices with their start and end apart: 44, of which 4 were waited for; matrix products, arithmetic and copies ran while one was open for 11% of the time, Pallas kernels for 0%

profile of v1, /device:TPU:1, one launch (start us, length us, event | category | flops | bytes accessed | tf_op | source)
XLA Modules:
  0.0 863.3 jit_solution(11759537969766863169)
XLA Ops:
  11.5 2.1 collective-permute-start
  13.6 6.6 collective-permute-start.1
  20.4 2.7 collective-permute-start.7
  26.0 2.5 collective-permute-start.2
  28.4 2.6 collective-permute-start.3
  41.6 2.0 mul.1238
  45.3 2.0 mul.1235
  48.9 1.9 mul.1232
  50.9 5.2 fusion.8
  56.1 2.0 reshape.697
  58.1 2.5 multiply_reduce_fusion.31
  60.6 4.7 collective-permute-start.11
  65.3 2.7 collective-permute-start.9
  76.7 10.3 %all-to-all-start.1 = ((s32[8,48,1]{1,2,0:T(1,128)}), s32[8,48,1]{1,2,0:T(1,128)}, u32[]{:S(2)}, u32[]{:S(2)}) async-start(s32[8,48,1]{1,2,0:T(1,128)} %sub.24), calls=%async_computation.1 | async-start | bytes 8192 | tf_op jit(solution)/shard_map/all_to_all | solution.py:77
  88.6 2.0 mul.1263
  92.3 2.0 mul.1267
  95.1 2.0 mul.1271
  98.7 2.0 mul.1275
  102.4 1.9 mul.1279
  106.0 2.0 mul.1283
  108.8 2.0 mul.1287
  111.7 2.0 mul.1259
  113.6 2.3 add_multiply_fusion.3
  119.7 4.8 all-to-all-start
  125.0 1.9 reduce.3
  130.0 2.3 reduce.4
  134.0 2.4 fusion.27
  136.5 138.2 %all-reduce.4.cloned.1.call-done = f32[64,1024]{1,0:T(8,128)} async-done(((f32[64,1024]{1,0:T(8,128)}), f32[64,1024]{1,0:T(8,128)}) %all-reduce.4.cloned.1.call-update) | async-done | bytes 262160 | tf_op jit(solution)/shard_map/psum | solution.py:110
  276.9 2.1 reshape.727
  279.0 15.2 %all_to_all.61 = f32[32,1,2048]{2,1,0:T(1,128)} all-to-all(f32[32,1,2048]{2,1,0:T(1,128)} %reshape.727), channel_id=1, replica_groups=mesh['sub'=32,'agg'=8] {'sub'}, dimensions={0} | all-to-all | bytes 524288 | tf_op jit(solution)/shard_map/all_to_all | solution.py:116
  294.2 2.8 reduce.5
  297.0 2.0 reshape.728
  299.0 2.6 fusion.82
  303.3 16.4 %all_to_all.62 = f32[8,1,3072]{2,1,0:T(1,128)} all-to-all(f32[8,1,3072]{2,1,0:T(1,128)} %reshape.729), channel_id=1, replica_groups=mesh['sub'=32,'agg'=8] {'agg'}, dimensions={0} | all-to-all | bytes 196608 | tf_op jit(solution)/shard_map/all_to_all | solution.py:119
  319.7 2.3 reduce.6
  325.2 4.0 fusion.23
  329.2 2.0 reshape.700
  331.2 3.2 multiply_reduce_fusion.23
  335.0 2.4 collective-permute-start.18
  337.4 2.8 collective-permute-start.17
  340.1 3.6 collective-permute-start.21
  343.7 2.7 collective-permute-start.23
  351.0 2.0 mul.1186
  369.6 3.9 multiply_reduce_fusion.42
  373.6 77.8 %all-reduce = (f32[64]{0:T(128)S(1)}, f32[64]{0:T(128)S(1)}) all-reduce(f32[64]{0:T(128)S(1)} %get-tuple-element.43, f32[64]{0:T(128)S(1)} %get-tuple-element.42), channel_id=1, replica_groups=mesh['sub'=32,'agg'=8] {'sub','agg'}, use_global_device_ids=true, to_apply=%region_17.18 | all-reduce | flops 128 | bytes 1024 | tf_op jit(solution)/shard_map/psum | solution.py:90
  452.5 3.2 fusion.11
  456.0 1.9 multiply_reduce_fusion.15
  458.8 2.4 collective-permute-start.26
  461.1 2.3 collective-permute-start.25
  463.5 3.5 collective-permute-start.29
  467.0 2.7 collective-permute-start.31
  479.4 1.8 multiply_reduce_fusion.41
  481.2 77.6 %psum.45 = f32[64]{0:T(128)S(1)} all-reduce(f32[64]{0:T(128)S(1)} %get-tuple-element.48), channel_id=1, replica_groups=mesh['sub'=32,'agg'=8] {'sub','agg'}, use_global_device_ids=true, to_apply=%region_41.42 | all-reduce | flops 64 | bytes 512 | tf_op jit(solution)/shard_map/psum | solution.py:90
  561.1 8.1 all_to_all.63
  571.6 137.1 %all-reduce.6.cloned.1.call-done = f32[64,1024]{1,0:T(8,128)} async-done(((f32[64,1024]{1,0:T(8,128)}), f32[64,1024]{1,0:T(8,128)}) %all-reduce.6.cloned.1.call-update) | async-done | bytes 262160 | tf_op jit(solution)/shard_map/psum | solution.py:110
  710.4 15.4 %all_to_all.64 = f32[32,1,2048]{2,1,0:T(1,128)S(1)} all-to-all(f32[32,1,2048]{2,1,0:T(1,128)S(1)} %reshape.733), channel_id=1, replica_groups=mesh['sub'=32,'agg'=8] {'sub'}, dimensions={0} | all-to-all | bytes 524288 | tf_op jit(solution)/shard_map/all_to_all | solution.py:116
  728.9 16.1 %all_to_all.65 = f32[8,1,3072]{2,1,0:T(1,128)S(1)} all-to-all(f32[8,1,3072]{2,1,0:T(1,128)S(1)} %reshape.735), channel_id=1, replica_groups=mesh['sub'=32,'agg'=8] {'agg'}, dimensions={0} | all-to-all | bytes 196608 | tf_op jit(solution)/shard_map/all_to_all | solution.py:119
  746.4 3.3 fusion.20
  752.2 2.4 collective-permute-start.34
  754.6 2.6 collective-permute-start.33
  757.2 3.6 collective-permute-start.37
  760.8 2.7 collective-permute-start.39
  774.9 2.0 multiply_reduce_fusion.40
  776.9 77.8 %psum.47 = f32[64]{0:T(128)S(1)} all-reduce(f32[64]{0:T(128)S(1)} %get-tuple-element.46), channel_id=1, replica_groups=mesh['sub'=32,'agg'=8] {'sub','agg'}, use_global_device_ids=true, to_apply=%region_52.53 | all-reduce | flops 64 | bytes 512 | tf_op jit(solution)/shard_map/psum | solution.py:127
  (321 shorter events, 116.5 us)
Async XLA Ops:
  7.2 108.8 %copy-start = (bf16[1,1,128,1536]{3,2,1,0:T(8,128)(2,1)S(1)}, bf16[1,1,128,1536]{3,2,1,0:T(8,128)(2,1)}, u32[]{:S(2)}) copy-start(bf16[1,1,128,1536]{3,2,1,0:T(8,128)(2,1)} %param.12) | copy-start | bytes 1179652
  9.9 23.9 %copy-start.40 = (f32[8]{0:T(128)}, f32[8]{0:T(128)S(1)}, u32[]{:S(2)}) copy-start(f32[8]{0:T(128)S(1)} %get-tuple-element.59) | copy-start | bytes 100
  9.9 24.1 %copy-start.43 = (f32[8]{0:T(128)}, f32[8]{0:T(128)S(1)}, u32[]{:S(2)}) copy-start(f32[8]{0:T(128)S(1)} %get-tuple-element.60) | copy-start | bytes 100
  9.9 25.3 %copy-start.27 = (f32[8]{0:T(128)}, f32[8]{0:T(128)S(1)}, u32[]{:S(2)}) copy-start(f32[8]{0:T(128)S(1)} %get-tuple-element.54) | copy-start | bytes 100
  9.9 25.3 %copy-start.29 = (f32[8]{0:T(128)}, f32[8]{0:T(128)S(1)}, u32[]{:S(2)}) copy-start(f32[8]{0:T(128)S(1)} %get-tuple-element.55) | copy-start | bytes 100
  9.9 25.3 %copy-start.31 = (f32[8]{0:T(128)}, f32[8]{0:T(128)S(1)}, u32[]{:S(2)}) copy-start(f32[8]{0:T(128)S(1)} %get-tuple-element.56) | copy-start | bytes 100
  9.9 25.3 %copy-start.46 = (f32[8]{0:T(128)}, f32[8]{0:T(128)S(1)}, u32[]{:S(2)}) copy-start(f32[8]{0:T(128)S(1)} %get-tuple-element.61) | copy-start | bytes 100
  11.5 35.7 %collective-permute-start = (f32[64,192]{1,0:T(8,128)S(1)}, f32[64,192]{1,0:T(8,128)}, u32[]{:S(2)}, u32[]{:S(2)}) collective-permute-start(f32[64,192]{1,0:T(8,128)S(1)} %get-tuple-element.2), channel_id=1, source_target_pairs={{248,0},{0,8},{8,16},{16,24},{24,32},{32,40},{40,48},{48,56},{56,6... | collective-permute-start | bytes 147464 | tf_op jit(solution)/shard_map/ppermute | solution.py:16
  13.6 30.0 %collective-permute-start.1 = (f32[64,192]{1,0:T(8,128)}, f32[64,192]{1,0:T(8,128)}, u32[]{:S(2)}, u32[]{:S(2)}) collective-permute-start(f32[64,192]{1,0:T(8,128)} %get-tuple-element.3), channel_id=1, source_target_pairs={{8,0},{16,8},{24,16},{32,24},{40,32},{48,40},{56,48},{64,56},{72,6... | collective-permute-start | bytes 147464 | tf_op jit(solution)/shard_map/ppermute | solution.py:16
  20.3 5.7 collective-permute-start.5
  20.4 8.1 collective-permute-start.6
  20.4 10.7 %collective-permute-start.7 = (f32[64,192]{1,0:T(8,128)S(1)}, f32[64,192]{1,0:T(8,128)S(1)}, u32[]{:S(2)}, u32[]{:S(2)}) collective-permute-start(f32[64,192]{1,0:T(8,128)S(1)} %get-tuple-element.9), channel_id=1, source_target_pairs={{32,0},{40,8},{48,16},{56,24},{64,32},{72,40},{80,48},{88,56},{96,... | collective-permute-start | bytes 147464 | tf_op jit(solution)/shard_map/ppermute | solution.py:16
  26.0 14.0 %collective-permute-start.2 = (f32[64,192]{1,0:T(8,128)}, f32[64,192]{1,0:T(8,128)}, u32[]{:S(2)}, u32[]{:S(2)}) collective-permute-start(f32[64,192]{1,0:T(8,128)} %get-tuple-element.4), channel_id=1, source_target_pairs={{240,0},{248,8},{0,16},{8,24},{16,32},{24,40},{32,48},{40,56},{48,... | collective-permute-start | bytes 147464 | tf_op jit(solution)/shard_map/ppermute | solution.py:16
  28.4 9.7 %collective-permute-start.3 = (f32[64,192]{1,0:T(8,128)S(1)}, f32[64,192]{1,0:T(8,128)}, u32[]{:S(2)}, u32[]{:S(2)}) collective-permute-start(f32[64,192]{1,0:T(8,128)S(1)} %get-tuple-element.5), channel_id=1, source_target_pairs={{16,0},{24,8},{32,16},{40,24},{48,32},{56,40},{64,48},{72,56},{80,... | collective-permute-start | bytes 147464 | tf_op jit(solution)/shard_map/ppermute | solution.py:16
  31.1 6.1 collective-permute-start.4
  60.6 8.4 collective-permute-start.11
  65.3 6.7 collective-permute-start.10
  65.3 8.3 collective-permute-start.9
  68.8 42.1 %collective-permute-start.8 = (f32[64,192]{1,0:T(8,128)S(1)}, f32[64,192]{1,0:T(8,128)S(1)}, u32[]{:S(2)}, u32[]{:S(2)}) collective-permute-start(f32[64,192]{1,0:T(8,128)S(1)} %get-tuple-element.34), channel_id=1, source_target_pairs={{248,0},{0,8},{8,16},{16,24},{24,32},{32,40},{40,48},{48,56},{56,6... | collective-permute-start | bytes 147464 | tf_op jit(solution)/shard_map/ppermute | solution.py:16
  68.8 39.1 %collective-permute-start.15 = (f32[64,192]{1,0:T(8,128)S(1)}, f32[64,192]{1,0:T(8,128)S(1)}, u32[]{:S(2)}, u32[]{:S(2)}) collective-permute-start(f32[64,192]{1,0:T(8,128)S(1)} %get-tuple-element.35), channel_id=1, source_target_pairs={{32,0},{40,8},{48,16},{56,24},{64,32},{72,40},{80,48},{88,56},{96,... | collective-permute-start | bytes 147464 | tf_op jit(solution)/shard_map/ppermute | solution.py:16
  68.9 35.4 %collective-permute-start.14 = (f32[64,192]{1,0:T(8,128)S(1)}, f32[64,192]{1,0:T(8,128)}, u32[]{:S(2)}, u32[]{:S(2)}) collective-permute-start(f32[64,192]{1,0:T(8,128)S(1)} %get-tuple-element.36), channel_id=1, source_target_pairs={{224,0},{232,8},{240,16},{248,24},{0,32},{8,40},{16,48},{24,56},{3... | collective-permute-start | bytes 147464 | tf_op jit(solution)/shard_map/ppermute | solution.py:16
  72.0 28.7 %collective-permute-start.13 = (f32[64,192]{1,0:T(8,128)S(1)}, f32[64,192]{1,0:T(8,128)}, u32[]{:S(2)}, u32[]{:S(2)}) collective-permute-start(f32[64,192]{1,0:T(8,128)S(1)} %get-tuple-element.37), channel_id=1, source_target_pairs={{24,0},{32,8},{40,16},{48,24},{56,32},{64,40},{72,48},{80,56},{88,... | collective-permute-start | bytes 147464 | tf_op jit(solution)/shard_map/ppermute | solution.py:16
  73.6 23.5 %collective-permute-start.12 = (f32[64,192]{1,0:T(8,128)S(1)}, f32[64,192]{1,0:T(8,128)}, u32[]{:S(2)}, u32[]{:S(2)}) collective-permute-start(f32[64,192]{1,0:T(8,128)S(1)} %get-tuple-element.38), channel_id=1, source_target_pairs={{232,0},{240,8},{248,16},{0,24},{8,32},{16,40},{24,48},{32,56},{40... | collective-permute-start | bytes 147464 | tf_op jit(solution)/shard_map/ppermute | solution.py:16
  76.7 43.0 %all-to-all-start.1 = ((s32[8,48,1]{1,2,0:T(1,128)}), s32[8,48,1]{1,2,0:T(1,128)}, u32[]{:S(2)}, u32[]{:S(2)}) async-start(s32[8,48,1]{1,2,0:T(1,128)} %sub.24), calls=%async_computation.1 | async-start | bytes 8192 | tf_op jit(solution)/shard_map/all_to_all | solution.py:77
  108.8 165.9 %copy-start.9 = (f32[1,32,1024]{2,1,0:T(8,128)S(1)}, f32[1,32,1024]{2,1,0:T(8,128)}, u32[]{:S(2)}) copy-start(f32[1,32,1024]{2,1,0:T(8,128)} %param.17) | copy-start | bytes 393220
  119.7 9.9 %all-to-all-start = ((f32[8,1,3072]{2,1,0:T(1,128)}), f32[8,1,3072]{2,1,0:T(1,128)}, u32[]{:S(2)}, u32[]{:S(2)}) async-start(f32[8,1,3072]{2,1,0:T(1,128)} %reshape.725), calls=%async_computation | async-start | bytes 196608 | tf_op jit(solution)/shard_map/all_to_all | solution.py:106
  124.5 150.3 %all-reduce.4.cloned.1.call-start = ((), (), s32[]{:S(2)}) async-start(), calls=%async_computation.7 | async-start | bytes 524288 | tf_op jit(solution)/shard_map/psum | solution.py:110
  136.4 572.2 %all-reduce.6.cloned.1.call-start = ((), (), s32[]{:S(2)}) async-start(), calls=%async_computation.8 | async-start | bytes 524288 | tf_op jit(solution)/shard_map/psum | solution.py:110
  334.4 9.3 %collective-permute-start.19 = (f32[64,192]{1,0:T(8,128)S(1)}, f32[64,192]{1,0:T(8,128)}, u32[]{:S(2)}, u32[]{:S(2)}) collective-permute-start(f32[64,192]{1,0:T(8,128)S(1)} %get-tuple-element.31), channel_id=1, source_target_pairs={{16,0},{24,8},{32,16},{40,24},{48,32},{56,40},{64,48},{72,56},{80,... | collective-permute-start | bytes 147464 | tf_op jit(solution)/shard_map/ppermute | solution.py:16
  335.0 8.7 %collective-permute-start.18 = (f32[64,192]{1,0:T(8,128)S(1)}, f32[64,192]{1,0:T(8,128)}, u32[]{:S(2)}, u32[]{:S(2)}) collective-permute-start(f32[64,192]{1,0:T(8,128)S(1)} %get-tuple-element.32), channel_id=1, source_target_pairs={{240,0},{248,8},{0,16},{8,24},{16,32},{24,40},{32,48},{40,56},{48,... | collective-permute-start | bytes 147464 | tf_op jit(solution)/shard_map/ppermute | solution.py:16
  337.4 9.0 %collective-permute-start.17 = (f32[64,192]{1,0:T(8,128)S(1)}, f32[64,192]{1,0:T(8,128)}, u32[]{:S(2)}, u32[]{:S(2)}) collective-permute-start(f32[64,192]{1,0:T(8,128)S(1)} %get-tuple-element.33), channel_id=1, source_target_pairs={{8,0},{16,8},{24,16},{32,24},{40,32},{48,40},{56,48},{64,56},{72,6... | collective-permute-start | bytes 147464 | tf_op jit(solution)/shard_map/ppermute | solution.py:16
  340.1 20.3 %collective-permute-start.20 = (f32[64,192]{1,0:T(8,128)}, f32[64,192]{1,0:T(8,128)}, u32[]{:S(2)}, u32[]{:S(2)}) collective-permute-start(f32[64,192]{1,0:T(8,128)} %get-tuple-element.30), channel_id=1, source_target_pairs={{232,0},{240,8},{248,16},{0,24},{8,32},{16,40},{24,48},{32,56},{40... | collective-permute-start | bytes 147464 | tf_op jit(solution)/shard_map/ppermute | solution.py:16
  340.1 22.1 %collective-permute-start.21 = (f32[64,192]{1,0:T(8,128)}, f32[64,192]{1,0:T(8,128)}, u32[]{:S(2)}, u32[]{:S(2)}) collective-permute-start(f32[64,192]{1,0:T(8,128)} %get-tuple-element.29), channel_id=1, source_target_pairs={{24,0},{32,8},{40,16},{48,24},{56,32},{64,40},{72,48},{80,56},{88,... | collective-permute-start | bytes 147464 | tf_op jit(solution)/shard_map/ppermute | solution.py:16
  343.7 20.4 %collective-permute-start.22 = (f32[64,192]{1,0:T(8,128)}, f32[64,192]{1,0:T(8,128)}, u32[]{:S(2)}, u32[]{:S(2)}) collective-permute-start(f32[64,192]{1,0:T(8,128)} %get-tuple-element.28), channel_id=1, source_target_pairs={{224,0},{232,8},{240,16},{248,24},{0,32},{8,40},{16,48},{24,56},{3... | collective-permute-start | bytes 147464 | tf_op jit(solution)/shard_map/ppermute | solution.py:16
  343.7 22.2 %collective-permute-start.23 = (f32[64,192]{1,0:T(8,128)}, f32[64,192]{1,0:T(8,128)}, u32[]{:S(2)}, u32[]{:S(2)}) collective-permute-start(f32[64,192]{1,0:T(8,128)} %get-tuple-element.27), channel_id=1, source_target_pairs={{32,0},{40,8},{48,16},{56,24},{64,32},{72,40},{80,48},{88,56},{96,... | collective-permute-start | bytes 147464 | tf_op jit(solution)/shard_map/ppermute | solution.py:16
  346.4 21.3 %collective-permute-start.16 = (f32[64,192]{1,0:T(8,128)}, f32[64,192]{1,0:T(8,128)}, u32[]{:S(2)}, u32[]{:S(2)}) collective-permute-start(f32[64,192]{1,0:T(8,128)} %get-tuple-element.26), channel_id=1, source_target_pairs={{248,0},{0,8},{8,16},{16,24},{24,32},{32,40},{40,48},{48,56},{56,6... | collective-permute-start | bytes 147464 | tf_op jit(solution)/shard_map/ppermute | solution.py:16
  373.6 82.4 %copy-start.28 = (f32[8]{0:T(128)S(1)}, f32[8]{0:T(128)}, u32[]{:S(2)}) copy-start(f32[8]{0:T(128)} %copy-done.27) | copy-start | bytes 100
  373.6 82.4 %copy-start.30 = (f32[8]{0:T(128)S(1)}, f32[8]{0:T(128)}, u32[]{:S(2)}) copy-start(f32[8]{0:T(128)} %copy-done.29) | copy-start | bytes 100
  373.6 82.4 %copy-start.32 = (f32[8]{0:T(128)S(1)}, f32[8]{0:T(128)}, u32[]{:S(2)}) copy-start(f32[8]{0:T(128)} %copy-done.31) | copy-start | bytes 100
  373.6 82.4 %copy-start.35 = (f32[8]{0:T(128)S(1)}, f32[8]{0:T(128)}, u32[]{:S(2)}) copy-start(f32[8]{0:T(128)} %copy-done.34) | copy-start | bytes 100
  373.6 82.4 %copy-start.38 = (f32[8]{0:T(128)S(1)}, f32[8]{0:T(128)}, u32[]{:S(2)}) copy-start(f32[8]{0:T(128)} %copy-done.37) | copy-start | bytes 100
  373.6 82.4 %copy-start.41 = (f32[8]{0:T(128)S(1)}, f32[8]{0:T(128)}, u32[]{:S(2)}) copy-start(f32[8]{0:T(128)} %copy-done.40) | copy-start | bytes 100
  373.6 82.4 %copy-start.44 = (f32[8]{0:T(128)S(1)}, f32[8]{0:T(128)}, u32[]{:S(2)}) copy-start(f32[8]{0:T(128)} %copy-done.43) | copy-start | bytes 100
  373.6 82.4 %copy-start.47 = (f32[8]{0:T(128)S(1)}, f32[8]{0:T(128)}, u32[]{:S(2)}) copy-start(f32[8]{0:T(128)} %copy-done.46) | copy-start | bytes 100
  457.9 9.0 %collective-permute-start.27 = (f32[64,192]{1,0:T(8,128)S(1)}, f32[64,192]{1,0:T(8,128)S(1)}, u32[]{:S(2)}, u32[]{:S(2)}) collective-permute-start(f32[64,192]{1,0:T(8,128)S(1)} %get-tuple-element.23), channel_id=1, source_target_pairs={{16,0},{24,8},{32,16},{40,24},{48,32},{56,40},{64,48},{72,56},{80,... | collective-permute-start | bytes 147464 | tf_op jit(solution)/shard_map/ppermute | solution.py:16
  458.8 8.3 collective-permute-start.26
  461.1 8.6 collective-permute-start.25
  463.4 6.9 collective-permute-start.28
  463.5 8.7 %collective-permute-start.29 = (f32[64,192]{1,0:T(8,128)}, f32[64,192]{1,0:T(8,128)}, u32[]{:S(2)}, u32[]{:S(2)}) collective-permute-start(f32[64,192]{1,0:T(8,128)} %get-tuple-element.21), channel_id=1, source_target_pairs={{24,0},{32,8},{40,16},{48,24},{56,32},{64,40},{72,48},{80,56},{88,... | collective-permute-start | bytes 147464 | tf_op jit(solution)/shard_map/ppermute | solution.py:16
  467.0 7.0 collective-permute-start.30
  467.0 8.8 %collective-permute-start.31 = (f32[64,192]{1,0:T(8,128)}, f32[64,192]{1,0:T(8,128)}, u32[]{:S(2)}, u32[]{:S(2)}) collective-permute-start(f32[64,192]{1,0:T(8,128)} %get-tuple-element.19), channel_id=1, source_target_pairs={{32,0},{40,8},{48,16},{56,24},{64,32},{72,40},{80,48},{88,56},{96,... | collective-permute-start | bytes 147464 | tf_op jit(solution)/shard_map/ppermute | solution.py:16
  469.7 7.9 collective-permute-start.24
  477.6 92.5 %copy-start.49 = (s32[384]{0:T(512)S(1)}, s32[384]{0:T(512)}, u32[]{:S(2)}) copy-start(s32[384]{0:T(512)} %eq.283) | copy-start | bytes 4612
  558.9 187.0 %copy-start.53 = (f32[64]{0:T(128)}, f32[64]{0:T(128)S(1)}, u32[]{:S(2)}) copy-start(f32[64]{0:T(128)S(1)} %psum.45) | copy-start | bytes 772
  559.5 186.3 %copy-start.50 = (s32[128]{0:T(128)S(1)}, s32[128]{0:T(128)}, u32[]{:S(2)}) copy-start(s32[128]{0:T(128)} %multiply_add_fusion.1) | copy-start | bytes 1540
  751.6 9.2 %collective-permute-start.35 = (f32[64,192]{1,0:T(8,128)S(1)}, f32[64,192]{1,0:T(8,128)S(1)}, u32[]{:S(2)}, u32[]{:S(2)}) collective-permute-start(f32[64,192]{1,0:T(8,128)S(1)} %get-tuple-element.15), channel_id=1, source_target_pairs={{16,0},{24,8},{32,16},{40,24},{48,32},{56,40},{64,48},{72,56},{80,... | collective-permute-start | bytes 147464 | tf_op jit(solution)/shard_map/ppermute | solution.py:16
  752.2 8.6 collective-permute-start.34
  754.6 8.9 %collective-permute-start.33 = (f32[64,192]{1,0:T(8,128)S(1)}, f32[64,192]{1,0:T(8,128)S(1)}, u32[]{:S(2)}, u32[]{:S(2)}) collective-permute-start(f32[64,192]{1,0:T(8,128)S(1)} %get-tuple-element.17), channel_id=1, source_target_pairs={{8,0},{16,8},{24,16},{32,24},{40,32},{48,40},{56,48},{64,56},{72,6... | collective-permute-start | bytes 147464 | tf_op jit(solution)/shard_map/ppermute | solution.py:16
  757.2 8.7 %collective-permute-start.36 = (f32[64,192]{1,0:T(8,128)}, f32[64,192]{1,0:T(8,128)}, u32[]{:S(2)}, u32[]{:S(2)}) collective-permute-start(f32[64,192]{1,0:T(8,128)} %get-tuple-element.14), channel_id=1, source_target_pairs={{232,0},{240,8},{248,16},{0,24},{8,32},{16,40},{24,48},{32,56},{40... | collective-permute-start | bytes 147464 | tf_op jit(solution)/shard_map/ppermute | solution.py:16
  757.2 10.5 %collective-permute-start.37 = (f32[64,192]{1,0:T(8,128)}, f32[64,192]{1,0:T(8,128)}, u32[]{:S(2)}, u32[]{:S(2)}) collective-permute-start(f32[64,192]{1,0:T(8,128)} %get-tuple-element.13), channel_id=1, source_target_pairs={{24,0},{32,8},{40,16},{48,24},{56,32},{64,40},{72,48},{80,56},{88,... | collective-permute-start | bytes 147464 | tf_op jit(solution)/shard_map/ppermute | solution.py:16
  760.8 8.7 %collective-permute-start.38 = (f32[64,192]{1,0:T(8,128)S(1)}, f32[64,192]{1,0:T(8,128)}, u32[]{:S(2)}, u32[]{:S(2)}) collective-permute-start(f32[64,192]{1,0:T(8,128)S(1)} %get-tuple-element.12), channel_id=1, source_target_pairs={{224,0},{232,8},{240,16},{248,24},{0,32},{8,40},{16,48},{24,56},{3... | collective-permute-start | bytes 147464 | tf_op jit(solution)/shard_map/ppermute | solution.py:16
  760.8 10.5 %collective-permute-start.39 = (f32[64,192]{1,0:T(8,128)S(1)}, f32[64,192]{1,0:T(8,128)}, u32[]{:S(2)}, u32[]{:S(2)}) collective-permute-start(f32[64,192]{1,0:T(8,128)S(1)} %get-tuple-element.11), channel_id=1, source_target_pairs={{32,0},{40,8},{48,16},{56,24},{64,32},{72,40},{80,48},{88,56},{96,... | collective-permute-start | bytes 147464 | tf_op jit(solution)/shard_map/ppermute | solution.py:16
  763.5 9.6 %collective-permute-start.32 = (f32[64,192]{1,0:T(8,128)S(1)}, f32[64,192]{1,0:T(8,128)}, u32[]{:S(2)}, u32[]{:S(2)}) collective-permute-start(f32[64,192]{1,0:T(8,128)S(1)} %get-tuple-element.10), channel_id=1, source_target_pairs={{248,0},{0,8},{8,16},{16,24},{24,32},{32,40},{40,48},{48,56},{56,6... | collective-permute-start | bytes 147464 | tf_op jit(solution)/shard_map/ppermute | solution.py:16
  768.6 86.7 %copy-start.52 = (f32[64]{0:T(128)S(1)}, f32[64]{0:T(128)}, u32[]{:S(2)}) copy-start(f32[64]{0:T(128)} %copy-done.51) | copy-start | bytes 772
  (35 other events, 478.0 us)
Sparse Core Ops, SparseCore 0:
  136.6 138.1 all-reduce.3
  571.7 136.9 all-reduce.5
